TPU v7x, 32 devices: a whole 2x2x4 slice. The times are simulated.
32 devices in a mesh: seq: 8 (over z, x), head: 4 (over y, core).
Axes of the slice: x: 2, y: 2, z: 4, core: 2. Of those that a mesh axis runs over, the one named last changes fastest.
Arguments:
- hidden_states: bfloat16 [2, 352, 5120], P(None, 'seq', 'head'), may hold values from -60 to 60
- clean_states: bfloat16 [2, 352, 5120], P(None, 'seq', 'head'), may hold values from -60 to 60
- w_query: bfloat16 [5120, 2560], P(None, 'head'), may hold values from -2 to 2
- w_key: bfloat16 [5120, 2560], P(None, 'head'), may hold values from -2 to 2
- w_value: bfloat16 [5120, 2560], P(None, 'head'), may hold values from -0.078125 to 0.078125
- q_gain: float32 [2560], P('head'), may hold values from 0.1 to 1.9
- k_gain: float32 [2560], P('head'), may hold values from 0.1 to 1.9
- cache_keys: bfloat16 [9, 352, 2560], P(None, 'seq', 'head'), may hold values from -1300 to 1300
- cache_values: bfloat16 [9, 352, 2560], P(None, 'seq', 'head'), may hold values from -6 to 6
- modulation: float32 [4, 2, 5120], replicated, may hold values from -3 to 3
- controls: int32 [3], replicated, may hold values from 0 to 6, as said below
- frame_pos: int32 [11], replicated, may hold values from 0 to 63
Outputs:
- attention_out: bfloat16 [2, 352, 2560], P(None, 'seq', 'head')
- new_keys: bfloat16 [9, 352, 2560], P(None, 'seq', 'head')
- new_values: bfloat16 [9, 352, 2560], P(None, 'seq', 'head')
Inputs may be any that keep to these rules, and one draw needn't show every extreme that they name: controls[0] lies in 1 to 3, controls[1] in 0 to 6 and equal to 6 whenever controls[0] is below 3, controls[2] in 1 to 2.
All inputs are finite; a program needn't handle non-finite values.
Results may differ from a plain program's by a relative error of at most 0.011.
The roundings to bfloat16 on the way count: a program that leaves them out, or rounds other values in their place, can miss the bound.
Values may be sent and summed in bfloat16 or wider, within the bound.
A program may use at most 320 MiB of HBM per device.

v0:
```python
import jax
import jax.numpy as jnp
from jax import lax
from jax.sharding import PartitionSpec as P

HD = 128
epsilon = 1e-06


def modulate(states, modulation, step_index):
    choose = (jnp.arange(modulation.shape[0], dtype=jnp.int32) == step_index).astype(jnp.float32)
    picked = jnp.sum(choose[:, None, None] * modulation, axis=0)
    values = states.astype(jnp.float32)
    centre = jnp.mean(values, axis=-1, keepdims=True)
    spread = jnp.mean(jnp.square(values - centre), axis=-1, keepdims=True)
    normed = (values - centre) * lax.rsqrt(spread + epsilon)
    return (normed * (1.0 + picked[1]) + picked[0]).astype(jnp.bfloat16)


def rms_scale(values, square_total, width, gain):
    return values * lax.rsqrt(square_total / width + epsilon)[:, None] * gain


def rotate(values, time_pos, space_pos):
    head_size = values.shape[-1]
    half_size = head_size // 2
    time_pairs = (head_size - 4 * (head_size // 6)) // 2
    space_pairs = half_size - time_pairs
    pair_index = jnp.arange(half_size, dtype=jnp.int32)
    exponent = jnp.where(
        pair_index < time_pairs, pair_index / time_pairs, (pair_index - time_pairs) / space_pairs
    ).astype(jnp.float32)
    frequency = jnp.power(10000.0, -exponent)
    is_time = (pair_index < time_pairs)[None, None, :]
    position = jnp.where(
        is_time,
        time_pos.astype(jnp.float32)[:, None, None],
        space_pos.astype(jnp.float32)[None, :, None],
    )
    angle = position * frequency
    cosine = jnp.cos(angle)[:, :, None, :]
    sine = jnp.sin(angle)[:, :, None, :]
    first = values[..., :half_size]
    second = values[..., half_size:]
    return jnp.concatenate(
        [first * cosine - second * sine, second * cosine + first * sine], axis=-1
    )


def write_cache(key_store, value_store, fresh_keys, fresh_values, slot_start, sinks):
    rolling = key_store.shape[0] - sinks
    for group_frame in range(fresh_keys.shape[0]):
        target = sinks + (slot_start + group_frame) % rolling
        anchor = (target, jnp.int32(0), jnp.int32(0))
        key_store = lax.dynamic_update_slice(
            key_store, fresh_keys[group_frame : group_frame + 1], anchor
        )
        value_store = lax.dynamic_update_slice(
            value_store, fresh_values[group_frame : group_frame + 1], anchor
        )
    return (key_store, value_store)


def body(
    hidden_states,
    clean_states,
    w_query,
    w_key,
    w_value,
    q_gain,
    k_gain,
    cache_keys,
    cache_values,
    modulation,
    controls,
    frame_pos,
):
    timestep = controls[0]
    write_slot = controls[1]
    sink_count = controls[2]
    full_hidden, full_clean = (
        lax.all_gather(hidden_states, "head", axis=2, tiled=True),
        lax.all_gather(clean_states, "head", axis=2, tiled=True),
    )
    group_count, local_frame, model_width = full_hidden.shape
    local_rows = group_count * local_frame
    cache_count = cache_keys.shape[0]
    local_inner = w_query.shape[1]
    head_size = HD
    local_heads = local_inner // head_size
    inner_width = local_inner * lax.axis_size("head")
    noisy = modulate(full_hidden, modulation, timestep).reshape(local_rows, model_width)
    settled = modulate(full_clean, modulation, jnp.int32(0)).reshape(local_rows, model_width)
    query_raw = jnp.dot(noisy, w_query, preferred_element_type=jnp.float32)
    key_raw = jnp.dot(noisy, w_key, preferred_element_type=jnp.float32)
    key_clean = jnp.dot(settled, w_key, preferred_element_type=jnp.float32)
    value_new = jnp.dot(noisy, w_value, preferred_element_type=jnp.float32).astype(jnp.bfloat16)
    value_clean = jnp.dot(settled, w_value, preferred_element_type=jnp.float32).astype(jnp.bfloat16)
    square_query, square_key, square_clean = lax.psum(
        (
            jnp.sum(query_raw * query_raw, axis=-1),
            jnp.sum(key_raw * key_raw, axis=-1),
            jnp.sum(key_clean * key_clean, axis=-1),
        ),
        "head",
    )
    query_norm = rms_scale(query_raw, square_query, inner_width, q_gain)
    key_norm = rms_scale(key_raw, square_key, inner_width, k_gain)
    stored_keys = rms_scale(key_clean, square_clean, inner_width, k_gain).astype(jnp.bfloat16)
    space_pos = lax.axis_index("seq") * local_frame + jnp.arange(local_frame, dtype=jnp.int32)
    group_time = frame_pos[cache_count:]
    cache_time = frame_pos[:cache_count]
    query_rot = (
        rotate(
            query_norm.reshape(group_count, local_frame, local_heads, head_size),
            group_time,
            space_pos,
        )
        .astype(jnp.bfloat16)
        .reshape(group_count, local_frame, local_inner)
    )
    key_rot = (
        rotate(
            key_norm.reshape(group_count, local_frame, local_heads, head_size),
            group_time,
            space_pos,
        )
        .astype(jnp.bfloat16)
        .reshape(group_count, local_frame, local_inner)
    )
    cache_rot = (
        rotate(
            cache_keys.astype(jnp.float32).reshape(
                cache_count, local_frame, local_heads, head_size
            ),
            cache_time,
            space_pos,
        )
        .astype(jnp.bfloat16)
        .reshape(cache_count, local_frame, local_inner)
    )
    key_local = jnp.concatenate([cache_rot, key_rot], axis=0)
    value_local = jnp.concatenate(
        [cache_values, value_new.reshape(group_count, local_frame, local_inner)], axis=0
    )
    scale = head_size ** (-0.5)
    query_whole = lax.all_gather(query_rot, "seq", axis=1, tiled=True)
    all_rows = query_whole.shape[0] * query_whole.shape[1]
    scores = (
        jnp.einsum(
            "qhd,khd->hqk",
            query_whole.reshape(all_rows, local_heads, head_size),
            key_local.reshape(-1, local_heads, head_size),
            preferred_element_type=jnp.float32,
        )
        * scale
    )
    top_score = lax.pmax(jnp.max(scores, axis=-1), "seq")
    weights = jnp.exp(scores - top_score[..., None])
    totals = jnp.sum(weights, axis=-1)
    summed = jnp.einsum(
        "hqk,khd->qhd",
        weights.astype(jnp.bfloat16),
        value_local.reshape(-1, local_heads, head_size),
        preferred_element_type=jnp.float32,
    )
    summed_part, totals_part = (
        lax.psum_scatter(
            summed.reshape(group_count, -1, local_inner), "seq", scatter_dimension=1, tiled=True
        ),
        lax.psum_scatter(
            jnp.transpose(totals).reshape(group_count, -1, local_heads),
            "seq",
            scatter_dimension=1,
            tiled=True,
        ),
    )
    attended = (
        summed_part.reshape(local_rows, local_heads, head_size)
        / totals_part.reshape(local_rows, local_heads)[:, :, None]
    )
    attention_out = attended.reshape(group_count, local_frame, local_inner).astype(jnp.bfloat16)
    new_keys, new_values = write_cache(
        cache_keys,
        cache_values,
        stored_keys.reshape(group_count, local_frame, local_inner),
        value_clean.reshape(group_count, local_frame, local_inner),
        write_slot,
        sink_count,
    )
    return (attention_out, new_keys, new_values)


def solution(mesh):
    in_specs = (
        P(None, "seq", "head"),
        P(None, "seq", "head"),
        P(None, "head"),
        P(None, "head"),
        P(None, "head"),
        P("head"),
        P("head"),
        P(None, "seq", "head"),
        P(None, "seq", "head"),
        P(),
        P(),
        P(),
    )
    out_specs = (P(None, "seq", "head"), P(None, "seq", "head"), P(None, "seq", "head"))
    return jax.shard_map(body, mesh=mesh, in_specs=in_specs, out_specs=out_specs, check_vma=False)
```

profile of v0, /device:TPU:0, one launch (start us, length us, event | category | flops | bytes accessed | tf_op | source)
XLA Modules:
  0.0 270.5 jit_solution(3133796648397645756)
XLA Ops:
  7.2 1.9 copy.76
  9.2 1.1 copy.77
  11.9 1.6 fusion.26
  13.5 10.7 %all_gather.9 = bf16[2,44,5120]{2,0,1:T(2,128)(2,1)S(1)} all-gather(bf16[2,44,1280]{2,0,1:T(2,128)(2,1)S(1)} %copy-done.4), channel_id=1, replica_groups=mesh['seq'=8,'head'=4] {'head'}, dimensions={2}, use_global_device_ids=true | all-gather | bytes 1126400 | tf_op jit(solution)/shard_map/all_gather | solution.py:82
  25.0 1.3 fusion.14
  26.6 1.7 fusion.17
  28.8 4.0 %convolution_convert_fusion.1 = bf16[88,640]{1,0:T(8,128)(2,1)S(1)} fusion(bf16[88,5120]{1,0:T(8,128)(2,1)S(1)} %reshape.149, bf16[5120,640]{1,0:T(8,128)(2,1)} %param.16), kind=kOutput, calls=%fused_computation.27 | convolution fusion | flops 576773120 | bytes 7567360 | tf_op jit(solution)/shard_map/dot_general | solution.py:97
  32.8 4.2 %multiply_reduce_fusion.2 = (f32[88]{0:T(128)S(1)}, f32[88,640]{1,0:T(8,128)S(1)}) fusion(bf16[88,5120]{1,0:T(8,128)(2,1)S(1)} %reshape.149, bf16[5120,640]{1,0:T(8,128)(2,1)} %param.15), kind=kOutput, calls=%fused_computation.43 | convolution fusion | flops 576829376 | bytes 7680352 | tf_op jit(solution)/shard_map/dot_general | solution.py:95
  37.0 4.2 %multiply_reduce_fusion.3 = (f32[88]{0:T(128)S(1)}, f32[88,640]{1,0:T(8,128)S(1)}) fusion(bf16[88,5120]{1,0:T(8,128)(2,1)S(1)} %reshape.149, bf16[5120,640]{1,0:T(8,128)(2,1)} %param.14), kind=kOutput, calls=%fused_computation.45 | convolution fusion | flops 576829376 | bytes 7680352 | tf_op jit(solution)/shard_map/dot_general | solution.py:94
  41.3 1.7 reshape.151
  42.9 9.5 %all_gather.11 = bf16[2,44,5120]{2,0,1:T(2,128)(2,1)S(1)} all-gather(bf16[2,44,1280]{2,0,1:T(2,128)(2,1)S(1)} %copy-done.5), channel_id=1, replica_groups=mesh['seq'=8,'head'=4] {'head'}, dimensions={2}, use_global_device_ids=true | all-gather | bytes 1126400 | tf_op jit(solution)/shard_map/all_gather | solution.py:83
  53.2 1.3 fusion.10
  54.5 1.7 fusion.13
  56.7 4.2 %multiply_reduce_fusion.1 = (f32[88]{0:T(128)S(1)}, f32[88,640]{1,0:T(8,128)S(1)}) fusion(bf16[88,5120]{1,0:T(8,128)(2,1)S(1)} %reshape.160, bf16[5120,640]{1,0:T(8,128)(2,1)} %param.15), kind=kOutput, calls=%fused_computation.41 | convolution fusion | flops 576829376 | bytes 7680352 | tf_op jit(solution)/shard_map/dot_general | solution.py:96
  60.8 6.7 %all-reduce.2 = (f32[88]{0:T(128)S(1)}, f32[88]{0:T(128)S(1)}, f32[88]{0:T(128)S(1)}) all-reduce(f32[88]{0:T(128)S(1)} %get-tuple-element.38, f32[88]{0:T(128)S(1)} %get-tuple-element.40, f32[88]{0:T(128)S(1)} %get-tuple-element.42), channel_id=1, replica_groups=mesh['seq'=8,'head'=4] {'head'}, use_global_device_ids=true, to_apply=%region_4.0 | all-reduce | flops 264 | bytes 2112 | tf_op jit(solution)/shard_map/psum | solution.py:99
  69.0 0.8 reshape.164
  70.2 33.1 %all_gather.10 = bf16[2,352,640]{2,0,1:T(2,128)(2,1)S(1)} all-gather(bf16[2,44,640]{2,0,1:T(2,128)(2,1)S(1)} %copy.56), channel_id=1, replica_groups=mesh['seq'=8,'head'=4] {'seq'}, dimensions={1}, use_global_device_ids=true | all-gather | bytes 1013760 | tf_op jit(solution)/shard_map/all_gather | solution.py:147
  103.3 1.7 copy.43
  105.8 1.6 reshape.162
  107.4 1.7 subtract_convert_fusion
  110.3 1.7 reshape.157
  112.0 5.6 %multiply_reduce_fusion = (f32[5,704]{1,0:T(8,128)S(1)}, f32[5,704,484]{2,1,0:T(8,128)}) fusion(bf16[704,5,128]{0,2,1:T(8,128)(2,1)S(1)} %reshape.153, bf16[484,5,128]{2,1,0:T(8,128)(2,1)} %reshape.157), kind=kOutput, calls=%fused_computation.1 | convolution fusion | flops 439545920 | bytes 8349440 | tf_op jit(solution)/shard_map/qhd,khd->hqk/dot_general | solution.py:150
  117.7 36.5 %pmax.7 = f32[5,704]{1,0:T(8,128)S(1)} all-reduce(f32[5,704]{1,0:T(8,128)S(1)} %get-tuple-element.44), channel_id=1, replica_groups=mesh['seq'=8,'head'=4] {'seq'}, use_global_device_ids=true, to_apply=%region_8.0 | all-reduce | flops 3520 | bytes 28160 | tf_op jit(solution)/shard_map/pmax | solution.py:158
  154.2 5.7 %fusion.18 = f32[704,5,128]{2,0,1:T(8,128)} fusion(f32[5,704,484]{2,1,0:T(8,128)} %get-tuple-element.45, f32[5,704]{1,0:T(8,128)S(1)} %pmax.7, bf16[484,5,128]{2,1,0:T(8,128)(2,1)S(1)} %copy-done), kind=kOutput, calls=%fused_computation.25 | convolution fusion | flops 441253120 | bytes 9250560 | tf_op jit(solution)/shard_map/hqk,khd->qhd/dot_general | solution.py:161
  159.9 1.9 copy.49
  161.8 2.9 %reshape.158 = f32[2,352,640]{1,0,2:T(2,128)} reshape(f32[704,5,128]{0,2,1:T(8,128)S(1)} %copy.49) | data formatting | bytes 3604480 | tf_op jit(solution)/shard_map/reshape | solution.py:169
  164.7 4.7 %copy.50 = f32[2,352,640]{2,0,1:T(2,128)} copy(f32[2,352,640]{1,0,2:T(2,128)} %reshape.158) | data formatting | bytes 3604480 | tf_op jit(solution)/shard_map/reshape | solution.py:169
  172.4 4.8 %fusion = f32[5,704]{1,0:T(8,128)S(1)} fusion(f32[5,704,484]{2,1,0:T(8,128)} %get-tuple-element.45, f32[5,704]{1,0:T(8,128)S(1)} %pmax.7), kind=kLoop, calls=%fused_computation.2 | loop fusion | flops 5107520 | bytes 6842880 | tf_op jit(solution)/shard_map/reduce_sum | solution.py:160
  178.5 33.9 %all-reduce.1 = f32[2,352,5]{1,0,2:T(2,128)S(1)} all-reduce(f32[2,352,5]{1,0,2:T(2,128)S(1)} %reshape.159), channel_id=3, replica_groups=mesh['seq'=8,'head'=4] {'seq'}, use_global_device_ids=true, to_apply=%region_11.0.clone | all-reduce | flops 3520 | bytes 28160
  212.8 4.1 %convolution_convert_fusion = bf16[88,640]{1,0:T(8,128)(2,1)S(1)} fusion(bf16[88,5120]{1,0:T(8,128)(2,1)S(1)} %reshape.160, bf16[5120,640]{1,0:T(8,128)(2,1)} %param.16), kind=kOutput, calls=%fused_computation.26 | convolution fusion | flops 576773120 | bytes 7567360 | tf_op jit(solution)/shard_map/dot_general | solution.py:98
  219.5 42.4 %all-reduce.5.cloned.1.call-done = f32[2,352,640]{2,0,1:T(2,128)} async-done(((f32[2,352,640]{2,0,1:T(2,128)}), f32[2,352,640]{2,0,1:T(2,128)}) %all-reduce.5.cloned.1.call-update) | async-done | bytes 1802256
  261.9 1.0 constant_dynamic-slice_fusion.1
  (78 shorter events, 12.7 us)
Async XLA Ops:
  7.2 6.4 %copy-start.4 = (bf16[2,44,1280]{2,0,1:T(2,128)(2,1)S(1)}, bf16[2,44,1280]{2,0,1:T(2,128)(2,1)}, u32[]{:S(2)}) copy-start(bf16[2,44,1280]{2,0,1:T(2,128)(2,1)} %param.12) | copy-start | bytes 675844
  7.2 3.2 %copy-start.7 = (s32[3]{0:T(128)S(1)}, s32[3]{0:T(128)}, u32[]{:S(2)}) copy-start(s32[3]{0:T(128)} %param.22) | copy-start | bytes 40
  7.2 3.1 %copy-start.10 = (s32[11]{0:T(128)S(1)}, s32[11]{0:T(128)}, u32[]{:S(2)}) copy-start(s32[11]{0:T(128)} %param.23) | copy-start | bytes 136
  7.2 254.7 %all-reduce.5.cloned.1.call-start = ((), (), s32[]{:S(2)}) async-start(), calls=%async_computation | async-start | bytes 3604480
  10.2 30.9 %copy-start.1 = (bf16[9,44,640]{2,1,0:T(8,128)(2,1)}, bf16[9,44,640]{2,1,0:T(8,128)(2,1)S(1)}, u32[]{:S(2)}) copy-start(bf16[9,44,640]{2,1,0:T(8,128)(2,1)S(1)} %copy.77) | copy-start | bytes 1520644
  11.6 14.7 %copy-start.6 = (f32[4,2,5120]{2,1,0:T(2,128)S(1)}, f32[4,2,5120]{2,1,0:T(2,128)}, u32[]{:S(2)}) copy-start(f32[4,2,5120]{2,1,0:T(2,128)} %param.21) | copy-start | bytes 491524
  41.2 1.8 copy-start.5
  56.6 10.9 %copy-start.8 = (f32[640]{0:T(1024)S(1)}, f32[640]{0:T(1024)}, u32[]{:S(2)}) copy-start(f32[640]{0:T(1024)} %param.18) | copy-start | bytes 7684
  56.7 11.7 %copy-start.9 = (f32[640]{0:T(1024)S(1)}, f32[640]{0:T(1024)}, u32[]{:S(2)}) copy-start(f32[640]{0:T(1024)} %param.17) | copy-start | bytes 7684
  109.1 1.2 copy-start.3
  112.0 42.1 %copy-start = (bf16[484,5,128]{2,1,0:T(8,128)(2,1)S(1)}, bf16[484,5,128]{2,1,0:T(8,128)(2,1)}, u32[]{:S(2)}) copy-start(bf16[484,5,128]{2,1,0:T(8,128)(2,1)} %reshape.151) | copy-start | bytes 1858564
  172.4 4.9 %copy-start.11 = (u32[32]{0:T(128)S(1)}, u32[32]{0:T(128)}, u32[]{:S(2)}) copy-start(u32[32]{0:T(128)} %constant.61) | copy-start | bytes 388
  212.8 4.7 %copy-start.2 = (bf16[88,640]{1,0:T(8,128)(2,1)S(1)}, bf16[88,640]{1,0:T(8,128)(2,1)}, u32[]{:S(2)}) copy-start(bf16[88,640]{1,0:T(8,128)(2,1)} %get-tuple-element.29) | copy-start | bytes 337924
Sparse Core Ops, SparseCore 0:
  169.5 92.3 all-reduce.4
where the time goes:
time: 271 us; the launch traced here: 270 us
  blocking collectives  130 us (48%)
  waiting for transfers between devices  42.4 us (16%)
  matrix products  32 us (12%)
  local copies, waits for them, and re-layouts  28.4 us (10%)
  other arithmetic  19.3 us (7%)
  between operations  18.1 us (7%)
    unnamed x2, waiting for transfers between devices  42.4 us
    pmax x1, blocking collectives, body(): top_score = lax.pmax(jnp.max(scores, axis=-1), 'seq')  36.5 us
    unnamed x1, blocking collectives  33.9 us
    all_gather x1, blocking collectives, body(): query_whole = lax.all_gather(query_rot, 'seq', axis=1, tiled=True)  33.1 us
    all_gather x1, blocking collectives, body(): lax.all_gather(hidden_states, 'head', axis=2, tiled=True)  10.7 us
    all_gather x1, blocking collectives, body(): lax.all_gather(clean_states, 'head', axis=2, tiled=True)  9.48 us
    reshape x2, local copies, waits for them, and re-layouts, body(): summed.reshape(group_count, -1, local_inner)  7.56 us
    psum x1, blocking collectives, body(): lax.psum((jnp.sum(query_raw * query_raw, axis=-1), jnp.sum(key_raw * key_...  6.68 us
  transfers between devices with their start and end apart: 1, of which 1 were waited for; matrix products, arithmetic and copies ran while one was open for 5% of the time, Pallas kernels for 0%

commit v1 on v0

--- a/solution.py
+++ b/solution.py
@@ -144,7 +144,12 @@
         [cache_values, value_new.reshape(group_count, local_frame, local_inner)], axis=0
     )
     scale = head_size ** (-0.5)
-    query_whole = lax.all_gather(query_rot, "seq", axis=1, tiled=True)
+    ring = [query_rot]
+    for hop in range(7):
+        ring.append(lax.ppermute(ring[-1], "seq", [(dev, (dev + 1) % 8) for dev in range(8)]))
+    query_whole = jnp.roll(
+        jnp.concatenate(ring[::-1], axis=1), (lax.axis_index("seq") + 1) * ring[0].shape[1], axis=1
+    )
     all_rows = query_whole.shape[0] * query_whole.shape[1]
     scores = (
         jnp.einsum(

time: 271 us -> 285 us (1.052)
  waiting for transfers between devices: 42.4 us -> 79.9 us
  blocking collectives: 130 us -> 94 us
  local copies, waits for them, and re-layouts: 28.4 us -> 37.3 us
    all_gather x1 -> x0, blocking collectives: 33.1 us -> none  [body(): query_whole = lax.all_gather(query_rot, 'seq', axis=1, tiled=True)]
    ppermute x0 -> x7, waiting for transfers between devices: none -> 31.8 us  [body(): lax.ppermute(ring[-1], 'seq', [(dev, (dev + 1) % 8) for dev in range(8)])]
    unnamed x30 -> x53, local copies, waits for them, and re-layouts: 5.4 us -> 13.1 us
    unnamed x2, waiting for transfers between devices: 42.4 us -> 48.1 us
    pmax x1, blocking collectives: 36.5 us -> 33.3 us  [body(): top_score = lax.pmax(jnp.max(scores, axis=-1), 'seq')]
  transfers between devices with their start and end apart: 1 -> 8, of which waited for: 1 -> 8; matrix products, arithmetic and copies ran while one was open for 5% -> 10% of each run, Pallas kernels for 0% -> 0%
where the time goes in v1:
time: 285 us; the launch traced here: 284 us
  blocking collectives  94 us (33%)
  waiting for transfers between devices  79.9 us (28%)
  local copies, waits for them, and re-layouts  37.3 us (13%)
  matrix products  33.8 us (12%)
  between operations  18.6 us (7%)
  other arithmetic  18.3 us (6%)
    unnamed x2, waiting for transfers between devices  48.1 us
    unnamed x1, blocking collectives  33.8 us
    pmax x1, blocking collectives, body(): top_score = lax.pmax(jnp.max(scores, axis=-1), 'seq')  33.3 us
    ppermute x7, waiting for transfers between devices, body(): lax.ppermute(ring[-1], 'seq', [(dev, (dev + 1) % 8) for dev in range(8)])  31.8 us
    unnamed x53, local copies, waits for them, and re-layouts  13.1 us
    all_gather x1, blocking collectives, body(): lax.all_gather(hidden_states, 'head', axis=2, tiled=True)  10.7 us
    all_gather x1, blocking collectives, body(): lax.all_gather(clean_states, 'head', axis=2, tiled=True)  9.5 us
    reshape x2, local copies, waits for them, and re-layouts, body(): summed.reshape(group_count, -1, local_inner)  7.71 us
  transfers between devices with their start and end apart: 8, of which 8 were waited for; matrix products, arithmetic and copies ran while one was open for 10% of the time, Pallas kernels for 0%

profile of v1, /device:TPU:0, one launch (start us, length us, event | category | flops | bytes accessed | tf_op | source)
XLA Modules:
  0.0 283.8 jit_solution(8100875769576238494)
XLA Ops:
  7.2 1.9 copy.93
  9.2 1.9 copy.94
  12.5 10.7 %all_gather.6 = bf16[2,44,5120]{2,0,1:T(2,128)(2,1)S(1)} all-gather(bf16[2,44,1280]{2,0,1:T(2,128)(2,1)S(1)} %copy-done.6), channel_id=1, replica_groups=mesh['seq'=8,'head'=4] {'head'}, dimensions={2}, use_global_device_ids=true | all-gather | bytes 1126400 | tf_op jit(solution)/shard_map/all_gather | solution.py:82
  25.7 1.8 fusion.17
  27.8 4.2 %multiply_reduce_fusion.2 = (f32[88]{0:T(128)S(1)}, f32[88,640]{1,0:T(8,128)S(1)}) fusion(bf16[88,5120]{1,0:T(8,128)(2,1)S(1)} %reshape.149, bf16[5120,640]{1,0:T(8,128)(2,1)} %param.15), kind=kOutput, calls=%fused_computation.43 | convolution fusion | flops 576829376 | bytes 7680352 | tf_op jit(solution)/shard_map/dot_general | solution.py:95
  32.0 4.2 %multiply_reduce_fusion.3 = (f32[88]{0:T(128)S(1)}, f32[88,640]{1,0:T(8,128)S(1)}) fusion(bf16[88,5120]{1,0:T(8,128)(2,1)S(1)} %reshape.149, bf16[5120,640]{1,0:T(8,128)(2,1)} %param.14), kind=kOutput, calls=%fused_computation.45 | convolution fusion | flops 576829376 | bytes 7680352 | tf_op jit(solution)/shard_map/dot_general | solution.py:94
  36.2 9.5 %all_gather.7 = bf16[2,44,5120]{2,0,1:T(2,128)(2,1)S(1)} all-gather(bf16[2,44,1280]{2,0,1:T(2,128)(2,1)S(1)} %copy-done.7), channel_id=1, replica_groups=mesh['seq'=8,'head'=4] {'head'}, dimensions={2}, use_global_device_ids=true | all-gather | bytes 1126400 | tf_op jit(solution)/shard_map/all_gather | solution.py:83
  47.8 1.8 fusion.13
  50.0 4.5 %multiply_reduce_fusion.1 = (f32[88]{0:T(128)S(1)}, f32[88,640]{1,0:T(8,128)S(1)}) fusion(bf16[88,5120]{1,0:T(8,128)(2,1)S(1)} %reshape.160, bf16[5120,640]{1,0:T(8,128)(2,1)} %param.15), kind=kOutput, calls=%fused_computation.41 | convolution fusion | flops 576829376 | bytes 7680352 | tf_op jit(solution)/shard_map/dot_general | solution.py:96
  54.5 6.7 %all-reduce.2 = (f32[88]{0:T(128)S(1)}, f32[88]{0:T(128)S(1)}, f32[88]{0:T(128)S(1)}) all-reduce(f32[88]{0:T(128)S(1)} %get-tuple-element.38, f32[88]{0:T(128)S(1)} %get-tuple-element.40, f32[88]{0:T(128)S(1)} %get-tuple-element.42), channel_id=1, replica_groups=mesh['seq'=8,'head'=4] {'head'}, use_global_device_ids=true, to_apply=%region_4.0 | all-reduce | flops 264 | bytes 2112 | tf_op jit(solution)/shard_map/psum | solution.py:99
  65.3 4.7 %convolution_convert_fusion.1 = bf16[88,640]{1,0:T(8,128)(2,1)} fusion(bf16[88,5120]{1,0:T(8,128)(2,1)S(1)} %reshape.149, bf16[5120,640]{1,0:T(8,128)(2,1)} %param.16), kind=kOutput, calls=%fused_computation.27 | convolution fusion | flops 576773120 | bytes 7567360 | tf_op jit(solution)/shard_map/dot_general | solution.py:97
  71.6 1.6 fusion.26
  74.9 4.0 %collective-permute-done.1 = bf16[2,44,640]{2,0,1:T(2,128)(2,1)} collective-permute-done((bf16[2,44,640]{2,0,1:T(2,128)(2,1)S(1)}, bf16[2,44,640]{2,0,1:T(2,128)(2,1)}, u32[]{:S(2)}, u32[]{:S(2)}) %collective-permute-start.1) | collective-permute-done | bytes 112672 | tf_op jit(solution)/shard_map/ppermute | solution.py:149
  78.9 1.7 subtract_convert_fusion
  84.9 1.8 collective-permute-done.2
  87.8 1.7 reshape.151
  89.5 5.3 %collective-permute-done.3 = bf16[2,44,640]{2,0,1:T(2,128)(2,1)S(1)} collective-permute-done((bf16[2,44,640]{2,0,1:T(2,128)(2,1)}, bf16[2,44,640]{2,0,1:T(2,128)(2,1)S(1)}, u32[]{:S(2)}, u32[]{:S(2)}) %collective-permute-start.3) | collective-permute-done | bytes 112672 | tf_op jit(solution)/shard_map/ppermute | solution.py:149
  95.0 8.5 %collective-permute-done.4 = bf16[2,44,640]{2,0,1:T(2,128)(2,1)} collective-permute-done((bf16[2,44,640]{2,0,1:T(2,128)(2,1)S(1)}, bf16[2,44,640]{2,0,1:T(2,128)(2,1)}, u32[]{:S(2)}, u32[]{:S(2)}) %collective-permute-start.4) | collective-permute-done | bytes 112672 | tf_op jit(solution)/shard_map/ppermute | solution.py:149
  104.7 6.6 %collective-permute-done.5 = bf16[2,44,640]{2,0,1:T(2,128)(2,1)S(1)} collective-permute-done((bf16[2,44,640]{2,0,1:T(2,128)(2,1)}, bf16[2,44,640]{2,0,1:T(2,128)(2,1)S(1)}, u32[]{:S(2)}, u32[]{:S(2)}) %collective-permute-start.5) | collective-permute-done | bytes 112672 | tf_op jit(solution)/shard_map/ppermute | solution.py:149
  111.4 1.7 reshape.157
  114.4 4.4 %collective-permute-done.6 = bf16[2,44,640]{2,0,1:T(2,128)(2,1)S(1)} collective-permute-done((bf16[2,44,640]{2,0,1:T(2,128)(2,1)S(1)}, bf16[2,44,640]{2,0,1:T(2,128)(2,1)S(1)}, u32[]{:S(2)}, u32[]{:S(2)}) %collective-permute-start.6) | collective-permute-done | bytes 112672 | tf_op jit(solution)/shard_map/ppermute | solution.py:149
  126.4 1.7 copy.43
  128.9 5.6 %multiply_reduce_fusion = (f32[5,704]{1,0:T(8,128)S(1)}, f32[5,704,484]{2,1,0:T(8,128)}) fusion(bf16[704,5,128]{0,2,1:T(8,128)(2,1)S(1)} %reshape.153, bf16[484,5,128]{2,1,0:T(8,128)(2,1)} %reshape.157), kind=kOutput, calls=%fused_computation.1 | convolution fusion | flops 439545920 | bytes 8349440 | tf_op jit(solution)/shard_map/qhd,khd->hqk/dot_general | solution.py:155
  134.6 33.3 %pmax.7 = f32[5,704]{1,0:T(8,128)S(1)} all-reduce(f32[5,704]{1,0:T(8,128)S(1)} %get-tuple-element.44), channel_id=1, replica_groups=mesh['seq'=8,'head'=4] {'seq'}, use_global_device_ids=true, to_apply=%region_8.0 | all-reduce | flops 3520 | bytes 28160 | tf_op jit(solution)/shard_map/pmax | solution.py:163
  167.9 5.7 %fusion.18 = f32[704,5,128]{2,0,1:T(8,128)} fusion(f32[5,704,484]{2,1,0:T(8,128)} %get-tuple-element.45, f32[5,704]{1,0:T(8,128)S(1)} %pmax.7, bf16[484,5,128]{2,1,0:T(8,128)(2,1)S(1)} %copy-done.1), kind=kOutput, calls=%fused_computation.25 | convolution fusion | flops 441253120 | bytes 9250560 | tf_op jit(solution)/shard_map/hqk,khd->qhd/dot_general | solution.py:166
  173.6 1.9 copy.49
  175.5 2.9 %reshape.158 = f32[2,352,640]{1,0,2:T(2,128)} reshape(f32[704,5,128]{0,2,1:T(8,128)S(1)} %copy.49) | data formatting | bytes 3604480 | tf_op jit(solution)/shard_map/reshape | solution.py:174
  178.4 4.8 %copy.50 = f32[2,352,640]{2,0,1:T(2,128)} copy(f32[2,352,640]{1,0,2:T(2,128)} %reshape.158) | data formatting | bytes 3604480 | tf_op jit(solution)/shard_map/reshape | solution.py:174
  183.3 4.9 %convolution_convert_fusion = bf16[88,640]{1,0:T(8,128)(2,1)S(1)} fusion(bf16[88,5120]{1,0:T(8,128)(2,1)} %copy-done, bf16[5120,640]{1,0:T(8,128)(2,1)} %param.16), kind=kOutput, calls=%fused_computation.26 | convolution fusion | flops 576773120 | bytes 7567360 | tf_op jit(solution)/shard_map/dot_general | solution.py:98
  190.7 2.0 fusion
  192.8 33.8 %all-reduce.1 = f32[2,352,5]{1,0,2:T(2,128)S(1)} all-reduce(f32[2,352,5]{1,0,2:T(2,128)S(1)} %reshape.159), channel_id=3, replica_groups=mesh['seq'=8,'head'=4] {'seq'}, use_global_device_ids=true, to_apply=%region_11.0.clone | all-reduce | flops 3520 | bytes 28160
  227.1 48.1 %all-reduce.5.cloned.1.call-done = f32[2,352,640]{2,0,1:T(2,128)} async-done(((f32[2,352,640]{2,0,1:T(2,128)}), f32[2,352,640]{2,0,1:T(2,128)}) %all-reduce.5.cloned.1.call-update) | async-done | bytes 1802256
  (117 shorter events, 31.4 us)
Async XLA Ops:
  7.2 5.4 %copy-start.6 = (bf16[2,44,1280]{2,0,1:T(2,128)(2,1)S(1)}, bf16[2,44,1280]{2,0,1:T(2,128)(2,1)}, u32[]{:S(2)}) copy-start(bf16[2,44,1280]{2,0,1:T(2,128)(2,1)} %param.12) | copy-start | bytes 675844
  7.2 4.0 %copy-start.9 = (s32[3]{0:T(128)S(1)}, s32[3]{0:T(128)}, u32[]{:S(2)}) copy-start(s32[3]{0:T(128)} %param.22) | copy-start | bytes 40
  7.2 3.9 %copy-start.12 = (s32[11]{0:T(128)S(1)}, s32[11]{0:T(128)}, u32[]{:S(2)}) copy-start(s32[11]{0:T(128)} %param.23) | copy-start | bytes 136
  7.2 268.0 %all-reduce.5.cloned.1.call-start = ((), (), s32[]{:S(2)}) async-start(), calls=%async_computation | async-start | bytes 3604480
  11.1 14.3 %copy-start.8 = (f32[4,2,5120]{2,1,0:T(2,128)S(1)}, f32[4,2,5120]{2,1,0:T(2,128)}, u32[]{:S(2)}) copy-start(f32[4,2,5120]{2,1,0:T(2,128)} %param.21) | copy-start | bytes 491524
  32.0 4.2 %copy-start.7 = (bf16[2,44,1280]{2,0,1:T(2,128)(2,1)S(1)}, bf16[2,44,1280]{2,0,1:T(2,128)(2,1)}, u32[]{:S(2)}) copy-start(bf16[2,44,1280]{2,0,1:T(2,128)(2,1)} %param.13) | copy-start | bytes 675844
  50.0 4.5 %copy-start = (bf16[88,5120]{1,0:T(8,128)(2,1)}, bf16[88,5120]{1,0:T(8,128)(2,1)S(1)}, u32[]{:S(2)}) copy-start(bf16[88,5120]{1,0:T(8,128)(2,1)S(1)} %reshape.160) | copy-start | bytes 2703364
  50.0 11.3 %copy-start.10 = (f32[640]{0:T(1024)S(1)}, f32[640]{0:T(1024)}, u32[]{:S(2)}) copy-start(f32[640]{0:T(1024)} %param.18) | copy-start | bytes 7684
  50.0 12.0 %copy-start.11 = (f32[640]{0:T(1024)S(1)}, f32[640]{0:T(1024)}, u32[]{:S(2)}) copy-start(f32[640]{0:T(1024)} %param.17) | copy-start | bytes 7684
  63.8 7.5 %collective-permute-start = (bf16[2,44,640]{2,0,1:T(2,128)(2,1)S(1)}, bf16[2,44,640]{2,0,1:T(2,128)(2,1)S(1)}, u32[]{:S(2)}, u32[]{:S(2)}) collective-permute-start(bf16[2,44,640]{2,0,1:T(2,128)(2,1)S(1)} %copy.56), channel_id=1, source_target_pairs={{0,4},{4,8},{8,12},{12,16},{16,20},{20,24},{24,28},{28,0},{1,5},{5... | collective-permute-start | bytes 337928 | tf_op jit(solution)/shard_map/ppermute | solution.py:149
  71.3 7.6 %copy-start.4 = (bf16[2,44,640]{2,0,1:T(2,128)(2,1)}, bf16[2,44,640]{2,0,1:T(2,128)(2,1)S(1)}, u32[]{:S(2)}) copy-start(bf16[2,44,640]{2,0,1:T(2,128)(2,1)S(1)} %collective-permute-done) | copy-start | bytes 337924
  71.3 7.6 %collective-permute-start.1 = (bf16[2,44,640]{2,0,1:T(2,128)(2,1)S(1)}, bf16[2,44,640]{2,0,1:T(2,128)(2,1)}, u32[]{:S(2)}, u32[]{:S(2)}) collective-permute-start(bf16[2,44,640]{2,0,1:T(2,128)(2,1)S(1)} %collective-permute-done), channel_id=1, source_target_pairs={{0,4},{4,8},{8,12},{12,16},{16,20},{20,24},{24,28},{28,0},{1,5},{5... | collective-permute-start | bytes 337928 | tf_op jit(solution)/shard_map/ppermute | solution.py:149
  78.9 7.8 %collective-permute-start.2 = (bf16[2,44,640]{2,0,1:T(2,128)(2,1)}, bf16[2,44,640]{2,0,1:T(2,128)(2,1)}, u32[]{:S(2)}, u32[]{:S(2)}) collective-permute-start(bf16[2,44,640]{2,0,1:T(2,128)(2,1)} %collective-permute-done.1), channel_id=1, source_target_pairs={{0,4},{4,8},{8,12},{12,16},{16,20},{20,24},{24,28},{28,0},{1,5},{5... | collective-permute-start | bytes 337928 | tf_op jit(solution)/shard_map/ppermute | solution.py:149
  80.6 14.2 %copy-start.2 = (bf16[2,44,5,64]{3,2,1,0:T(8,128)(2,1)S(1)}, bf16[2,44,5,64]{3,2,1,0:T(8,128)(2,1)}, u32[]{:S(2)}) copy-start(bf16[2,44,5,64]{3,2,1,0:T(8,128)(2,1)} %get-tuple-element.20) | copy-start | bytes 168964
  86.7 8.1 %collective-permute-start.3 = (bf16[2,44,640]{2,0,1:T(2,128)(2,1)}, bf16[2,44,640]{2,0,1:T(2,128)(2,1)S(1)}, u32[]{:S(2)}, u32[]{:S(2)}) collective-permute-start(bf16[2,44,640]{2,0,1:T(2,128)(2,1)} %collective-permute-done.2), channel_id=1, source_target_pairs={{0,4},{4,8},{8,12},{12,16},{16,20},{20,24},{24,28},{28,0},{1,5},{5... | collective-permute-start | bytes 337928 | tf_op jit(solution)/shard_map/ppermute | solution.py:149
  94.8 8.8 %collective-permute-start.4 = (bf16[2,44,640]{2,0,1:T(2,128)(2,1)S(1)}, bf16[2,44,640]{2,0,1:T(2,128)(2,1)}, u32[]{:S(2)}, u32[]{:S(2)}) collective-permute-start(bf16[2,44,640]{2,0,1:T(2,128)(2,1)S(1)} %collective-permute-done.3), channel_id=1, source_target_pairs={{0,4},{4,8},{8,12},{12,16},{16,20},{20,24},{24,28},{28,0},{1,5},{5... | collective-permute-start | bytes 337928 | tf_op jit(solution)/shard_map/ppermute | solution.py:149
  103.5 7.8 %collective-permute-start.5 = (bf16[2,44,640]{2,0,1:T(2,128)(2,1)}, bf16[2,44,640]{2,0,1:T(2,128)(2,1)S(1)}, u32[]{:S(2)}, u32[]{:S(2)}) collective-permute-start(bf16[2,44,640]{2,0,1:T(2,128)(2,1)} %collective-permute-done.4), channel_id=1, source_target_pairs={{0,4},{4,8},{8,12},{12,16},{16,20},{20,24},{24,28},{28,0},{1,5},{5... | collective-permute-start | bytes 337928 | tf_op jit(solution)/shard_map/ppermute | solution.py:149
  104.7 8.4 %copy-start.13 = (u32[32]{0:T(128)S(1)}, u32[32]{0:T(128)}, u32[]{:S(2)}) copy-start(u32[32]{0:T(128)} %constant.77) | copy-start | bytes 388
  111.3 7.5 %collective-permute-start.6 = (bf16[2,44,640]{2,0,1:T(2,128)(2,1)S(1)}, bf16[2,44,640]{2,0,1:T(2,128)(2,1)S(1)}, u32[]{:S(2)}, u32[]{:S(2)}) collective-permute-start(bf16[2,44,640]{2,0,1:T(2,128)(2,1)S(1)} %collective-permute-done.5), channel_id=1, source_target_pairs={{0,4},{4,8},{8,12},{12,16},{16,20},{20,24},{24,28},{28,0},{1,5},{5... | collective-permute-start | bytes 337928 | tf_op jit(solution)/shard_map/ppermute | solution.py:149
  111.4 10.7 %copy-start.5 = (bf16[2,44,640]{2,0,1:T(2,128)(2,1)S(1)}, bf16[2,44,640]{2,0,1:T(2,128)(2,1)}, u32[]{:S(2)}) copy-start(bf16[2,44,640]{2,0,1:T(2,128)(2,1)} %copy-done.4) | copy-start | bytes 337924
  128.9 38.9 %copy-start.1 = (bf16[484,5,128]{2,1,0:T(8,128)(2,1)S(1)}, bf16[484,5,128]{2,1,0:T(8,128)(2,1)}, u32[]{:S(2)}) copy-start(bf16[484,5,128]{2,1,0:T(8,128)(2,1)} %reshape.151) | copy-start | bytes 1858564
  178.4 12.3 %slice-start = ((s8[7208960]{0:T(1024)(128)(4,1)}), s8[3014656]{0:T(1024)(128)(4,1)S(1)}, s32[]{:S(2)}) async-start(s8[7208960]{0:T(1024)(128)(4,1)} %bitcast.50), calls=%async_computation.1 | async-start | bytes 6029312
  183.2 5.6 %copy-start.3 = (bf16[88,640]{1,0:T(8,128)(2,1)S(1)}, bf16[88,640]{1,0:T(8,128)(2,1)}, u32[]{:S(2)}) copy-start(bf16[88,640]{1,0:T(8,128)(2,1)} %get-tuple-element.29) | copy-start | bytes 337924
  183.2 7.5 %slice-start.1 = ((s8[7208960]{0:T(1024)(128)(4,1)}), s8[4194304]{0:T(1024)(128)(4,1)S(1)}, s32[]{:S(2)}) async-start(s8[7208960]{0:T(1024)(128)(4,1)} %bitcast.50), calls=%async_computation.2 | async-start | bytes 8388608
Sparse Core Ops, SparseCore 0:
  183.4 91.7 all-reduce.4
